TPU v7x, 256 devices: a 8x8x2 block of a 8x8x16 slice. The times are simulated.
256 devices in a mesh: beam: 2 (over z), tm: 16 (over x, core), dm: 8 (over y).
Axes of the slice: x: 8, y: 8, z: 2, core: 2. Of those that a mesh axis runs over, the one named last changes fastest.
The devices are a block of a 8x8x16 slice.
Arguments:
- series: float32 [32, 524288], P(('beam', 'dm'), 'tm'), parts along dimension 0, may hold values from -16 to 16
- cand_start: int32 [32, 8, 8, 16], P(('beam', 'tm'), 'dm'), parts along dimension 0, may hold values from 0 to 1920
- cand_count: int32 [32, 8, 8], P(('beam', 'tm'), 'dm'), parts along dimension 0, may hold values from 0 to 16, as said below
Outputs:
- harmonic_sum: float32 [32, 32768], P(('beam', 'dm'), 'tm'), parts along dimension 0
- sifted: float32 [32, 8, 8, 16, 128], P(('beam', 'tm'), 'dm'), parts along dimension 0
There are 2 independent parts, one for each index of `beam`. A program takes and returns all parts, laid end to end along the dimension named above; each array names one. Nothing has to cross between parts.
Inputs may be any that keep to these rules, and one draw needn't show every extreme that they name: `cand_count`: in every draw some destination band receives 16 live slots from every source band and frequency shard.
All inputs are finite; a program needn't handle non-finite values.
Results may differ from a plain program's by a relative error of at most 0.00015.
Values sent between devices are 32-bit elements; how exact they have to be, the bound alone decides.
A program may use at most 128 MiB of HBM per device.

v0:
```python
import functools
import math

import jax
import jax.numpy as jnp
import numpy as np
from jax import lax
from jax.experimental import pallas as pl
from jax.experimental.pallas import tpu as pltpu
from jax.sharding import PartitionSpec as P

HARM = 8
BW = 128
EPSILON = 1e-06
LANES = 128
RADIX = 16
JOBS = RADIX // 2
LEFT, RIGHT = 128, 256
MESH = pl.DeviceIdType.MESH
SLOT_RESIDUES = (1, 3, 5, 7, 9, 11, 13, 15, 2, 6, 10, 14, 4, 12, 8, 0)
HALF = JOBS


def tables(total):
    def wave(left, right, period):
        angle = 2.0 * math.pi * (np.outer(left, right) % period) / period
        return np.cos(angle), np.sin(angle)

    left, right, radix = np.arange(LEFT), np.arange(RIGHT), np.arange(RADIX)
    parts = [
        *wave(left, left, LEFT),
        *wave(left, right, LEFT * RIGHT),
        *wave(left, right, RIGHT),
        *wave(radix, left, RADIX * LEFT),
        *wave(radix, right, total),
    ]
    rows, offsets = [], []
    for part in parts:
        offsets.append(sum(r.shape[0] for r in rows))
        for lane in range(0, part.shape[1], LANES):
            rows.append(part[:, lane : lane + LANES])
    return np.concatenate(rows).astype(np.float32), offsets


def split(value):
    high = value.astype(jnp.bfloat16)
    return high, (value - high.astype(jnp.float32)).astype(jnp.bfloat16)


def split_exactly(value):
    high, rest = value.astype(jnp.bfloat16), None
    rest = value - high.astype(jnp.float32)
    middle = rest.astype(jnp.bfloat16)
    return high, middle, (rest - middle.astype(jnp.float32)).astype(jnp.bfloat16)


def dot(left, right, dims):
    return lax.dot_general(left, right, (dims, ((), ())), preferred_element_type=jnp.float32)


def dot_split(left, right, dims):
    (lh, ll), (rh, rl) = left, right
    return dot(lh, rh, dims) + (dot(ll, rh, dims) + dot(lh, rl, dims))


def radix_transform(x):
    half, quarter = RADIX // 2, RADIX // 4

    def real_transform(values, count):
        if count == 1:
            return [(values[0], None)]
        low = [values[i] + values[i + count // 2] for i in range(count // 2)]
        high = [values[i] - values[i + count // 2] for i in range(count // 2)]
        out = {2 * i: v for i, v in enumerate(real_transform(low, count // 2))}
        if count == 2:
            out[1] = (high[0], None)
        elif count == 4:
            out[1] = (high[0], -high[1])
        else:
            h, q = count // 2, count // 4
            minus = [None] + [high[i] - high[h - i] for i in range(1, q)]
            plus = [None] + [high[i] + high[h - i] for i in range(1, q)]
            for term in range(1, h, 2):
                re, im = high[0], high[q] * (-math.sin(2 * math.pi * q * term / count))
                for i in range(1, q):
                    re = re + minus[i] * math.cos(2 * math.pi * i * term / count)
                    im = im - plus[i] * math.sin(2 * math.pi * i * term / count)
                out[term] = (re, im)
        return [out[i] for i in range(count // 2 + 1)]

    return real_transform(x, RADIX)


def picks(job):
    pair = (0, RADIX // 2) if job == 0 else (job, RADIX - job)
    found = {}
    for slot, residue in enumerate(SLOT_RESIDUES):
        for harmonic in range(1, HARM + 1):
            product = harmonic * residue
            if product % RADIX in pair:
                found.setdefault(slot, []).append(
                    (pair.index(product % RADIX), harmonic, product // RADIX)
                )
    return found


def search_kernel(
    shards, bands, offsets, total,
    x_ref, start_ref, count_ref, tab_hbm,
    hsum_ref, diff_ref, mark_ref,
    tab, x_in, y_out, y_in, w_hi, w_lo, g_hi, g_lo, t_cos, t_sin, pw,
    h_out, h_in, st_out, st_in, mk_out, mk_in, pk_out, pk_in,
    send_x, recv_x, send_y, recv_y, send_h, recv_h, send_s, recv_s,
    send_m, recv_m, send_p, recv_p, local_sem,
):
    me = lax.axis_index("tm")
    band = lax.axis_index("dm")
    job, row_kept = me // 2, me % 2
    bins = total // 2
    x_rows = x_in.shape[1]

    barrier = pltpu.get_barrier_semaphore()
    for i in range(1, shards):
        pl.semaphore_signal(
            barrier, inc=1, device_id={"tm": lax.rem(me + i, shards)}, device_id_type=MESH
        )
    for i in range(1, bands):
        pl.semaphore_signal(
            barrier, inc=1, device_id={"dm": lax.rem(band + i, bands)}, device_id_type=MESH
        )
    pl.semaphore_wait(barrier, shards + bands - 2)

    def remote(src, dst, send, recv, axis, peer):
        return pltpu.make_async_remote_copy(
            src_ref=src, dst_ref=dst, send_sem=send, recv_sem=recv,
            device_id={axis: peer}, device_id_type=MESH,
        )

    def x_copy(peer, slot):
        rows = pl.ds(pl.multiple_of(peer * x_rows, x_rows), x_rows)
        return remote(x_ref.at[rows], x_in.at[slot], send_x.at[peer], recv_x.at[slot], "tm", peer)

    def y_copy(peer, slot):
        rows = pl.ds(pl.multiple_of(slot * 8, 8), 8)
        return remote(y_out.at[peer], y_in.at[:, rows], send_y.at[peer], recv_y.at[slot], "tm", peer)

    def h_copy(peer, slot, rows):
        part = pl.ds(0, rows)
        return remote(
            h_out.at[peer, part], h_in.at[slot, part], send_h.at[peer], recv_h.at[slot], "tm", peer
        )

    def s_copy(peer, slot):
        return remote(st_out, st_in.at[slot], send_s.at[peer], recv_s.at[slot], "tm", peer)

    def m_copy(peer, slot):
        return remote(mk_out.at[peer], mk_in.at[slot], send_m.at[peer], recv_m.at[slot], "dm", peer)

    def p_copy(peer, slot):
        return remote(pk_out, pk_in.at[slot], send_p.at[peer], recv_p.at[slot], "dm", peer)

    others = [lax.rem(me + i, shards) for i in range(1, shards)]
    other_bands = [lax.rem(band + i, bands) for i in range(1, bands)]

    for peer in others:
        x_copy(peer, me).start()
    own_rows = pl.ds(pl.multiple_of(me * x_rows, x_rows), x_rows)
    own_x = pltpu.make_async_copy(x_ref.at[own_rows], x_in.at[me], local_sem.at[0])
    own_x.start()
    get_tab = pltpu.make_async_copy(tab_hbm, tab, local_sem.at[1])
    get_tab.start()

    slots = start_ref.shape[1]
    starts = start_ref[...].astype(jnp.float32)
    starts = jnp.concatenate(
        [starts, jnp.full((bands, LANES - slots), -1.0, jnp.float32)], axis=1
    )
    lane_row = lax.broadcasted_iota(jnp.int32, (1, LANES), 1)
    for d in range(bands):
        mk_out[d] = jnp.where(lane_row < count_ref[d], starts[d : d + 1], -1.0)
    for peer in other_bands:
        m_copy(peer, band).start()
    mk_in[band] = mk_out[band]

    get_tab.wait()

    def table(index, rows):
        first = offsets[index]
        return tab[first : first + rows, :]

    def wide(index, rows):
        first = offsets[index]
        return jnp.concatenate(
            [tab[first : first + rows, :], tab[first + rows : first + 2 * rows, :]], axis=1
        )

    def wide_row(index, at):
        first = offsets[index]
        return jnp.concatenate(
            [tab[pl.ds(first + at, 1), :], tab[pl.ds(first + RADIX + at, 1), :]], axis=1
        )

    paired = jnp.where(job == 0, 0.0, 1.0).astype(jnp.float32)
    alone = 1.0 - paired
    residues = (job, jnp.where(job == 0, RADIX // 2, RADIX - job))
    waves = []
    for c, residue in enumerate(residues):
        bc, bs = table(0, LEFT), table(1, LEFT)
        vc = tab[pl.ds(offsets[6] + residue, 1), :]
        vs = tab[pl.ds(offsets[7] + residue, 1), :]
        waves.append((bc * vc - bs * vs, bs * vc + bc * vs))
        bc, bs = wide(2, LEFT), wide(3, LEFT)
        vc, vs = wide_row(8, residue), wide_row(9, residue)
        t_cos[c] = bc * vc - bs * vs
        t_sin[c] = bs * vc + bc * vs
    (ca, sa), (cb, sb) = waves
    blocks = (
        (ca, paired * sa),
        (-sa, paired * ca),
        (paired * cb, alone * cb - paired * sb),
        (-paired * sb, -alone * sb - paired * cb),
    )
    for i, block in enumerate(blocks):
        high, low = split(jnp.concatenate(block, axis=1))
        w_hi[LEFT * i : LEFT * (i + 1), :] = high
        w_lo[LEFT * i : LEFT * (i + 1), :] = low
    gc, gs = wide(4, LEFT), wide(5, LEFT)
    for i, block in enumerate(((gc, gs), (-gs, gc))):
        high, low = split(jnp.concatenate(block, axis=1))
        g_hi[LEFT * i : LEFT * (i + 1), :] = high
        g_lo[LEFT * i : LEFT * (i + 1), :] = low

    own_x.wait()
    for i in range(1, shards):
        slot = lax.rem(me + shards - i, shards)
        x_copy(slot, slot).wait_recv()
    for row in range(2):
        for side in range(RIGHT // LANES):
            pick = pl.ds(2 * side + row, 8, stride=4)
            terms = radix_transform([x_in[t, pick, :] for t in range(shards)])
            lanes = slice(side * LANES, (side + 1) * LANES)
            for j in range(JOBS):
                re, im = (terms[0][0], terms[JOBS][0]) if j == 0 else terms[j]
                y_out[2 * j + row, 0, :, lanes] = re
                y_out[2 * j + row, 1, :, lanes] = im
    for peer in others:
        y_copy(peer, me).start()
    y_in[:, pl.ds(pl.multiple_of(me * 8, 8), 8), :] = y_out[me]

    for i in range(1, bands):
        slot = lax.rem(band + bands - i, bands)
        m_copy(slot, slot).wait_recv()
    lane = lax.broadcasted_iota(jnp.int32, (slots, LANES), 1)
    slot_id = lax.broadcasted_iota(jnp.int32, (slots, LANES), 0)
    for d in range(bands):
        spread_row = jnp.broadcast_to(mk_in[d], (slots, LANES))
        column = jnp.sum(jnp.where(lane == slot_id, spread_row, 0.0), axis=1, keepdims=True)
        mark_ref[d] = jnp.broadcast_to(column, (slots, LANES))

    for i in range(1, shards):
        slot = lax.rem(me + shards - i, shards)
        y_copy(slot, slot).wait_recv()

    y = jnp.concatenate([y_in[0], y_in[1]], axis=0)
    u = dot_split((w_hi[...], w_lo[...]), split(y), ((1,), (0,)))
    turned = []
    for c in range(2):
        ur, ui = u[2 * c * LEFT : (2 * c + 1) * LEFT], u[(2 * c + 1) * LEFT : (2 * c + 2) * LEFT]
        turned.append(
            jnp.concatenate(
                [ur * t_cos[c] + ui * t_sin[c], ui * t_cos[c] - ur * t_sin[c]], axis=1
            )
        )
    v = jnp.concatenate(turned, axis=0)
    z = dot_split((g_hi[...], g_lo[...]), split(v), ((1,), (1,)))
    zr, zi = z[:LEFT], z[LEFT:]
    power = (zr * zr + zi * zi) * (1.0 / total)
    pw[0] = power[:, :LEFT]
    pw[1] = power[:, LEFT:]

    groups = LEFT * LEFT // (HARM * LANES)
    lane = lax.broadcasted_iota(jnp.int32, (groups, LANES), 1)

    def decimate(which, harmonic, offset, cache):
        if (which, harmonic) not in cache:
            cache[which, harmonic] = [
                pw[which, pl.ds(b, groups, stride=harmonic), :] if harmonic > 1 else pw[which, pl.ds(0, groups), :]
                for b in range(harmonic)
            ]
        rows = cache[which, harmonic]
        if harmonic == 1:
            return rows[0]
        place = lane * harmonic + offset
        index, block = place & (LANES - 1), place >> 7
        out = jnp.take_along_axis(rows[0], index, axis=1, mode="promise_in_bounds")
        for b in range(1, harmonic):
            got = jnp.take_along_axis(rows[b], index, axis=1, mode="promise_in_bounds")
            out = jnp.where(block == b, got, out)
        return out

    for j in range(JOBS):

        @pl.when(job == j)
        def _(j=j):
            cache = {}
            found = picks(j)
            slot_count = HALF if j % 2 else len(SLOT_RESIDUES)
            for slot in range(slot_count):
                acc = None
                for which, harmonic, offset in found.get(slot, []):
                    got = decimate(which, harmonic, offset, cache)
                    acc = got if acc is None else acc + got
                if acc is None:
                    acc = jnp.zeros((groups, LANES), jnp.float32)
                h_out[:, slot, :] = acc

    odd = job % 2 == 1

    @pl.when(odd)
    def _():
        for peer in others:
            h_copy(peer, me, HALF).start()
        h_in[me, :HALF] = h_out[me, :HALF]

    @pl.when(jnp.logical_not(odd))
    def _():
        for peer in others:
            h_copy(peer, me, 2 * HALF).start()
        h_in[me] = h_out[me]

    count = 2 * LEFT * LEFT
    mean = jnp.sum(power, keepdims=True).reshape(1, 1) * (1.0 / count)
    away = power - mean
    squares = jnp.sum(away * away, keepdims=True).reshape(1, 1)
    st_out[0:1, :] = jnp.broadcast_to(mean, (1, LANES))
    st_out[1:2, :] = jnp.broadcast_to(squares, (1, LANES))
    for peer in others:
        s_copy(peer, me).start()
    st_in[me] = st_out[...]

    for v in range(shards):

        @pl.when(v != me)
        def _(v=v):
            h_copy(v, v, HALF if (v // 2) % 2 else 2 * HALF).wait_recv()
            s_copy(v, v).wait_recv()

    rows_out = []
    for row in range(2):
        sources = [2 * j + row for j in range(JOBS)]
        stats = [st_in[v] for v in sources]
        mean = sum(s[0:1] for s in stats) * (1.0 / JOBS)
        squares = sum(s[1:2] for s in stats)
        between = sum((s[0:1] - mean) * (s[0:1] - mean) for s in stats)
        spread = (squares + between * float(count)) * (1.0 / bins)
        scale = 1.0 / jnp.sqrt(spread + EPSILON)
        first = sum(h_in[v, :HALF, :] for v in sources)
        second = sum(h_in[v, HALF:, :] for v in sources if (v // 2) % 2 == 0)
        summed = jnp.concatenate([first, second], axis=0)
        rows_out.append((summed - float(HARM) * mean) * scale)

    both = jnp.concatenate(rows_out, axis=1)
    stacked = jnp.concatenate([p.astype(jnp.float32) for p in split_exactly(both)], axis=0).astype(jnp.bfloat16)
    places = stacked.shape[0]
    slot_at = lax.broadcasted_iota(jnp.int32, (places, LANES), 0) & (RADIX - 1)
    lane_at = lax.broadcasted_iota(jnp.int32, (places, LANES), 1) & (RADIX - 1)
    residue_of = jnp.where(
        slot_at < 8, 2 * slot_at + 1,
        jnp.where(slot_at < 12, 4 * slot_at - 30, jnp.where(slot_at < 14, 8 * slot_at - 92, jnp.where(slot_at == 14, 8, 0))),
    )
    chosen = (residue_of == lane_at).astype(jnp.float32).astype(jnp.bfloat16)
    laid = dot(stacked, chosen, ((0,), (0,)))
    at = lax.broadcasted_iota(jnp.int32, laid.shape, 0) & (LANES // RADIX - 1)
    lane = lax.broadcasted_iota(jnp.int32, laid.shape, 1) >> 4
    laid = jnp.where(at == lane, laid, 0.0)
    laid = jnp.sum(laid.reshape(2 * groups, LANES // RADIX, LANES), axis=1)
    top, low = laid[:groups], laid[groups:]
    pk_out[...] = jnp.maximum(top, low)
    for peer in other_bands:
        p_copy(peer, band).start()
    hsum_ref[pl.ds(0, groups, stride=2), :] = top
    hsum_ref[pl.ds(1, groups, stride=2), :] = low
    level = (top + low) * 0.5
    pk_in[band] = pk_out[...]
    for i in range(1, bands):
        slot = lax.rem(band + bands - i, bands)
        p_copy(slot, slot).wait_recv()
    for d in range(bands):
        diff_ref[d] = pk_in[d] - level

    for peer in others:
        x_copy(peer, me).wait_send()
        y_copy(peer, me).wait_send()
        s_copy(peer, me).wait_send()

    @pl.when(odd)
    def _():
        for peer in others:
            h_copy(peer, me, HALF).wait_send()

    @pl.when(jnp.logical_not(odd))
    def _():
        for peer in others:
            h_copy(peer, me, 2 * HALF).wait_send()

    for peer in other_bands:
        m_copy(peer, band).wait_send()
        p_copy(peer, band).wait_send()


def sift_kernel(bands, hsum_ref, diff_ref, mark_ref, out_h_ref, out_ref):
    out_h_ref[...] = hsum_ref[...]
    groups = diff_ref.shape[1]
    slots = mark_ref.shape[1]
    lane = lax.broadcasted_iota(jnp.int32, (slots, LANES), 1)
    for d in range(bands):
        mark = mark_ref[d].astype(jnp.int32)
        begin = jnp.maximum(mark, 0)
        row, shift = begin >> 7, begin & (LANES - 1)
        parts = [p.astype(jnp.float32) for p in split_exactly(diff_ref[d])]
        parts.append(jnp.zeros((LANES - 3 * groups, LANES), jnp.float32))
        source = jnp.concatenate(parts, axis=0).astype(jnp.bfloat16)
        live = lane < 3 * groups
        wanted = lane & (groups - 1)
        first = jnp.where(live & (wanted == row), 1.0, 0.0)
        second = jnp.where(live & (wanted == row + 1), 1.0, 0.0)
        choose = jnp.concatenate([first, second], axis=0).astype(jnp.bfloat16)
        pair = dot(choose, source, ((1,), (0,)))
        index = (lane + shift) & (LANES - 1)
        low = jnp.take_along_axis(pair[:slots], index, axis=1, mode="promise_in_bounds")
        high = jnp.take_along_axis(pair[slots:], index, axis=1, mode="promise_in_bounds")
        value = jnp.where(lane + shift < LANES, low, high)
        out_ref[d] = jnp.where(mark >= 0, value, 0.0)


def per_device(series, cand_start, cand_count):
    dm_rows, samples = series.shape
    shards, bands = lax.axis_size("tm"), lax.axis_size("dm")
    total = samples * shards
    slots = cand_start.shape[3]
    fundamentals = total // (2 * HARM) // shards
    assert shards == RADIX and dm_rows == 2 and samples == LEFT * RIGHT
    chunks = samples // LANES
    x = series.reshape(dm_rows, chunks, LANES).transpose(1, 0, 2).reshape(dm_rows * chunks, LANES)
    tab, offsets = tables(total)
    groups = fundamentals // LANES
    f32, bf16 = jnp.float32, jnp.bfloat16
    vmem = pl.BlockSpec(memory_space=pltpu.VMEM)
    hbm = pl.BlockSpec(memory_space=pl.ANY)
    dma = pltpu.SemaphoreType.DMA
    hsum, diff, mark = pl.pallas_call(
        functools.partial(search_kernel, shards, bands, tuple(offsets), total),
        name="search",
        out_shape=(
            jax.ShapeDtypeStruct((dm_rows * groups, LANES), f32),
            jax.ShapeDtypeStruct((bands, groups, LANES), f32),
            jax.ShapeDtypeStruct((bands, slots, LANES), f32),
        ),
        in_specs=[hbm, vmem, pl.BlockSpec(memory_space=pltpu.SMEM), hbm],
        out_specs=[vmem] * 3,
        scratch_shapes=[
            pltpu.VMEM(tab.shape, f32),
            pltpu.VMEM((shards, dm_rows * chunks // shards, LANES), f32),
            pltpu.VMEM((shards, 2, LEFT // shards, RIGHT), f32),
            pltpu.VMEM((2, LEFT, RIGHT), f32),
            pltpu.VMEM((4 * LEFT, 2 * LEFT), bf16),
            pltpu.VMEM((4 * LEFT, 2 * LEFT), bf16),
            pltpu.VMEM((2 * LEFT, 2 * RIGHT), bf16),
            pltpu.VMEM((2 * LEFT, 2 * RIGHT), bf16),
            pltpu.VMEM((2, LEFT, RIGHT), f32),
            pltpu.VMEM((2, LEFT, RIGHT), f32),
            pltpu.VMEM((2, LEFT, LEFT), f32),
            pltpu.VMEM((shards, 2 * HALF, LANES), f32),
            pltpu.VMEM((shards, 2 * HALF, LANES), f32),
            pltpu.VMEM((2, LANES), f32),
            pltpu.VMEM((shards, 2, LANES), f32),
            pltpu.VMEM((bands, 1, LANES), f32),
            pltpu.VMEM((bands, 1, LANES), f32),
            pltpu.VMEM((groups, LANES), f32),
            pltpu.VMEM((bands, groups, LANES), f32),
            *[dma((shards,)) for _ in range(8)],
            *[dma((bands,)) for _ in range(4)],
            dma((2,)),
        ],
        compiler_params=pltpu.CompilerParams(
            collective_id=0, has_side_effects=True, vmem_limit_bytes=32 << 20
        ),
    )(x, cand_start.reshape(bands, slots), cand_count.reshape(bands), jnp.asarray(tab))
    harmonic, sifted = pl.pallas_call(
        functools.partial(sift_kernel, bands),
        name="sift",
        out_shape=(
            jax.ShapeDtypeStruct(hsum.shape, f32),
            jax.ShapeDtypeStruct((bands, slots, BW), f32),
        ),
        in_specs=[vmem] * 3,
        out_specs=[vmem] * 2,
    )(hsum, diff, mark)
    harmonic = harmonic.reshape(groups, dm_rows, LANES).transpose(1, 0, 2)
    return harmonic.reshape(dm_rows, fundamentals), sifted[None, None]


def solution(mesh):
    return jax.shard_map(
        per_device,
        mesh=mesh,
        in_specs=(
            P(("beam", "dm"), "tm"),
            P(("beam", "tm"), "dm", None, None),
            P(("beam", "tm"), "dm", None),
        ),
        out_specs=(P(("beam", "dm"), "tm"), P(("beam", "tm"), "dm", None, None, None)),
        check_vma=False,
    )
```

profile of v0, /device:TPU:513, one launch (start us, length us, event | category | flops | bytes accessed | tf_op | source)
XLA Modules:
  0.0 57.6 jit_solution(711163720956657057)
XLA Ops:
  0.6 0.0 copy-start.5
  0.6 0.0 copy-start.6
  0.6 0.7 %copy-done.5 = s32[1,1,8,16]{3,2,1,0:T(8,128)S(1)} copy-done((s32[1,1,8,16]{3,2,1,0:T(8,128)S(1)}, s32[1,1,8,16]{3,2,1,0:T(8,128)}, u32[]{:S(2)}) %copy-start.5) | copy-done | bytes 536
  1.3 0.0 copy-done.6
  1.3 0.0 copy-start
  1.3 1.1 %copy-done = f32[1376,128]{1,0:T(8,128)S(1)} copy-done((f32[1376,128]{1,0:T(8,128)S(1)}, f32[1376,128]{1,0:T(8,128)}, u32[]{:S(2)}) %copy-start) | copy-done | bytes 704536
  2.4 0.0 copy-start.1
  2.4 0.9 %copy-done.1 = f32[2,32768]{1,0:T(2,128)S(1)} copy-done((f32[2,32768]{1,0:T(2,128)S(1)}, f32[2,32768]{1,0:T(2,128)}, u32[]{:S(2)}) %copy-start.1) | copy-done | bytes 262168
  3.4 50.5 %search.1 = (f32[32,128]{1,0:T(8,128)S(1)}, f32[8,16,128]{2,1,0:T(8,128)S(1)}, f32[8,16,128]{2,1,0:T(8,128)S(1)}) custom-call(f32[512,128]{1,0:T(8,128)S(1)} %bitcast.13, s32[8,16]{1,0:T(8,128)S(1)} %bitcast.14, s32[8]{0:T(128)S(1)} %bitcast.15, f32[1376,128]{1,0:T(8,128)S(1)} %copy-done), custom_call_target="tpu_custom_call" | custom-call | tf_op jit(solution)/shard_map/search/pallas_call | solution.py:451
  53.9 0.0 copy-start.2
  53.9 0.6 %copy-done.2 = f32[8,16,128]{2,1,0:T(8,128)} copy-done((f32[8,16,128]{2,1,0:T(8,128)}, f32[8,16,128]{2,1,0:T(8,128)S(1)}, u32[]{:S(2)}) %copy-start.2) | copy-done | bytes 65560
  54.5 0.0 copy-start.3
  54.5 0.6 %copy-done.3 = f32[8,16,128]{2,1,0:T(8,128)} copy-done((f32[8,16,128]{2,1,0:T(8,128)}, f32[8,16,128]{2,1,0:T(8,128)S(1)}, u32[]{:S(2)}) %copy-start.3) | copy-done | bytes 65560
  55.2 0.0 copy-start.4
  55.2 0.6 %copy-done.4 = f32[32,128]{1,0:T(8,128)} copy-done((f32[32,128]{1,0:T(8,128)}, f32[32,128]{1,0:T(8,128)S(1)}, u32[]{:S(2)}) %copy-start.4) | copy-done | bytes 16408
  55.8 1.8 %sift.1 = (f32[32,128]{1,0:T(8,128)}, f32[8,16,128]{2,1,0:T(8,128)}) custom-call(f32[32,128]{1,0:T(8,128)} %copy-done.4, f32[8,16,128]{2,1,0:T(8,128)} %copy-done.2, f32[8,16,128]{2,1,0:T(8,128)} %copy-done.3), custom_call_target="tpu_custom_call" | custom-call | tf_op jit(solution)/shard_map/sift/pallas_call | solution.py:489
Async XLA Ops:
  0.6 0.7 %copy-start.5 = (s32[1,1,8,16]{3,2,1,0:T(8,128)S(1)}, s32[1,1,8,16]{3,2,1,0:T(8,128)}, u32[]{:S(2)}) copy-start(s32[1,1,8,16]{3,2,1,0:T(8,128)} %param.5) | copy-start | bytes 1540
  0.6 0.7 %copy-start.6 = (s32[1,1,8]{2,1,0:T(1,128)S(1)}, s32[1,1,8]{2,1,0:T(1,128)}, u32[]{:S(2)}) copy-start(s32[1,1,8]{2,1,0:T(1,128)} %param.6) | copy-start | bytes 100
  1.3 1.1 %copy-start = (f32[1376,128]{1,0:T(8,128)S(1)}, f32[1376,128]{1,0:T(8,128)}, u32[]{:S(2)}) copy-start(f32[1376,128]{1,0:T(8,128)} %constant.2.clone.tab_hbm) | copy-start | bytes 2113540
  2.4 0.9 %copy-start.1 = (f32[2,32768]{1,0:T(2,128)S(1)}, f32[2,32768]{1,0:T(2,128)}, u32[]{:S(2)}) copy-start(f32[2,32768]{1,0:T(2,128)} %param.4) | copy-start | bytes 786436
  53.9 0.6 %copy-start.2 = (f32[8,16,128]{2,1,0:T(8,128)}, f32[8,16,128]{2,1,0:T(8,128)S(1)}, u32[]{:S(2)}) copy-start(f32[8,16,128]{2,1,0:T(8,128)S(1)} %get-tuple-element.8.diff_ref) | copy-start | bytes 196612
  54.5 0.6 %copy-start.3 = (f32[8,16,128]{2,1,0:T(8,128)}, f32[8,16,128]{2,1,0:T(8,128)S(1)}, u32[]{:S(2)}) copy-start(f32[8,16,128]{2,1,0:T(8,128)S(1)} %get-tuple-element.9.mark_ref) | copy-start | bytes 196612
  55.2 0.6 %copy-start.4 = (f32[32,128]{1,0:T(8,128)}, f32[32,128]{1,0:T(8,128)S(1)}, u32[]{:S(2)}) copy-start(f32[32,128]{1,0:T(8,128)S(1)} %get-tuple-element.7.hsum_ref) | copy-start | bytes 49156
where the time goes:
time: 58.2 us; the launch traced here: 57.6 us
  Pallas kernels  52.3 us (90%)
  local copies, waits for them, and re-layouts  4.58 us (8%)
  between operations  0.67 us (1%)
    pallas_call x1, Pallas kernels, per_device(): pl.pallas_call(functools.partial(search_kernel, shards, bands, tuple(offs...  50.5 us
    unnamed x14, local copies, waits for them, and re-layouts  4.58 us
    pallas_call x1, Pallas kernels, per_device(): pl.pallas_call(functools.partial(sift_kernel, bands), name='sift', out_sh...  1.79 us

commit v1 on v0

--- a/solution.py
+++ b/solution.py
@@ -104,14 +104,40 @@
     return found
 
 
+def far_first(count):
+    return sorted(range(1, count), key=lambda i: -min(i, count - i))
+
+
+def sift(bands, groups, slots, differences, marks, out_ref):
+    lane = lax.broadcasted_iota(jnp.int32, (slots, LANES), 1)
+    live = lane < 3 * groups
+    wanted = lane & (groups - 1)
+    for d in range(bands):
+        mark = marks[d]
+        begin = jnp.maximum(mark, 0)
+        row, shift = begin >> 7, begin & (LANES - 1)
+        parts = [p.astype(jnp.float32) for p in split_exactly(differences[d])]
+        parts.append(jnp.zeros((LANES - 3 * groups, LANES), jnp.float32))
+        source = jnp.concatenate(parts, axis=0).astype(jnp.bfloat16)
+        first = jnp.where(live & (wanted == row), 1.0, 0.0)
+        second = jnp.where(live & (wanted == row + 1), 1.0, 0.0)
+        choose = jnp.concatenate([first, second], axis=0).astype(jnp.bfloat16)
+        pair = dot(choose, source, ((1,), (0,)))
+        index = (lane + shift) & (LANES - 1)
+        low = jnp.take_along_axis(pair[:slots], index, axis=1, mode="promise_in_bounds")
+        high = jnp.take_along_axis(pair[slots:], index, axis=1, mode="promise_in_bounds")
+        value = jnp.where(lane + shift < LANES, low, high)
+        out_ref[d] = jnp.where(mark >= 0, value, 0.0)
+
+
 def search_kernel(
     shards, bands, offsets, total,
-    x_ref, start_ref, count_ref, tab_hbm,
-    hsum_ref, diff_ref, mark_ref,
-    tab, x_in, y_out, y_in, w_hi, w_lo, g_hi, g_lo, t_cos, t_sin, pw,
+    x_ref, start_hbm, count_hbm, tab_hbm,
+    hsum_ref, out_ref,
+    start_ref, count_ref, tab, x_in, y_out, y_in, w_hi, w_lo, g_hi, g_lo, t_cos, t_sin, pw,
     h_out, h_in, st_out, st_in, mk_out, mk_in, pk_out, pk_in,
     send_x, recv_x, send_y, recv_y, send_h, recv_h, send_s, recv_s,
-    send_m, recv_m, send_p, recv_p, local_sem,
+    send_m, recv_m, send_p, recv_p, local_sem, here_shard, here_band,
 ):
     me = lax.axis_index("tm")
     band = lax.axis_index("dm")
@@ -119,16 +145,29 @@
     bins = total // 2
     x_rows = x_in.shape[1]
 
+    first_shard, first_band = me == 0, band == 0
     barrier = pltpu.get_barrier_semaphore()
-    for i in range(1, shards):
-        pl.semaphore_signal(
-            barrier, inc=1, device_id={"tm": lax.rem(me + i, shards)}, device_id_type=MESH
-        )
-    for i in range(1, bands):
-        pl.semaphore_signal(
-            barrier, inc=1, device_id={"dm": lax.rem(band + i, bands)}, device_id_type=MESH
-        )
-    pl.semaphore_wait(barrier, shards + bands - 2)
+    others = [lax.rem(me + i, shards) for i in far_first(shards)]
+    other_bands = [lax.rem(band + i, bands) for i in far_first(bands)]
+
+    def greet(semaphore, axis, peers):
+        for peer in peers:
+            pl.semaphore_signal(semaphore, inc=1, device_id={axis: peer}, device_id_type=MESH)
+
+    @pl.when(jnp.logical_not(first_shard))
+    def _():
+        greet(barrier, "tm", others)
+
+    @pl.when(jnp.logical_not(first_band))
+    def _():
+        greet(barrier, "dm", other_bands)
+
+    late = first_shard.astype(jnp.int32) + first_band.astype(jnp.int32)
+    pl.semaphore_wait(barrier, shards + bands - 4 + late)
+
+    @pl.when(first_shard)
+    def _():
+        greet(here_shard, "tm", others)
 
     def remote(src, dst, send, recv, axis, peer):
         return pltpu.make_async_remote_copy(
@@ -159,18 +198,34 @@
     def p_copy(peer, slot):
         return remote(pk_out, pk_in.at[slot], send_p.at[peer], recv_p.at[slot], "dm", peer)
 
-    others = [lax.rem(me + i, shards) for i in range(1, shards)]
-    other_bands = [lax.rem(band + i, bands) for i in range(1, bands)]
-
     for peer in others:
-        x_copy(peer, me).start()
+
+        @pl.when(peer != 0)
+        def _(peer=peer):
+            x_copy(peer, me).start()
+
     own_rows = pl.ds(pl.multiple_of(me * x_rows, x_rows), x_rows)
     own_x = pltpu.make_async_copy(x_ref.at[own_rows], x_in.at[me], local_sem.at[0])
     own_x.start()
-    get_tab = pltpu.make_async_copy(tab_hbm, tab, local_sem.at[1])
+    get_starts = pltpu.make_async_copy(start_hbm, start_ref, local_sem.at[1])
+    get_starts.start()
+    get_counts = pltpu.make_async_copy(count_hbm, count_ref, local_sem.at[2])
+    get_counts.start()
+    get_tab = pltpu.make_async_copy(tab_hbm, tab, local_sem.at[3])
     get_tab.start()
 
+    @pl.when(first_band)
+    def _():
+        greet(here_band, "dm", other_bands)
+
+    @pl.when(jnp.logical_not(first_shard))
+    def _():
+        pl.semaphore_wait(here_shard, 1)
+        x_copy(0, me).start()
+
     slots = start_ref.shape[1]
+    get_starts.wait()
+    get_counts.wait()
     starts = start_ref[...].astype(jnp.float32)
     starts = jnp.concatenate(
         [starts, jnp.full((bands, LANES - slots), -1.0, jnp.float32)], axis=1
@@ -179,7 +234,11 @@
     for d in range(bands):
         mk_out[d] = jnp.where(lane_row < count_ref[d], starts[d : d + 1], -1.0)
     for peer in other_bands:
-        m_copy(peer, band).start()
+
+        @pl.when(peer != 0)
+        def _(peer=peer):
+            m_copy(peer, band).start()
+
     mk_in[band] = mk_out[band]
 
     get_tab.wait()
@@ -247,15 +306,10 @@
         y_copy(peer, me).start()
     y_in[:, pl.ds(pl.multiple_of(me * 8, 8), 8), :] = y_out[me]
 
-    for i in range(1, bands):
-        slot = lax.rem(band + bands - i, bands)
-        m_copy(slot, slot).wait_recv()
-    lane = lax.broadcasted_iota(jnp.int32, (slots, LANES), 1)
-    slot_id = lax.broadcasted_iota(jnp.int32, (slots, LANES), 0)
-    for d in range(bands):
-        spread_row = jnp.broadcast_to(mk_in[d], (slots, LANES))
-        column = jnp.sum(jnp.where(lane == slot_id, spread_row, 0.0), axis=1, keepdims=True)
-        mark_ref[d] = jnp.broadcast_to(column, (slots, LANES))
+    @pl.when(jnp.logical_not(first_band))
+    def _():
+        pl.semaphore_wait(here_band, 1)
+        m_copy(0, band).start()
 
     for i in range(1, shards):
         slot = lax.rem(me + shards - i, shards)
@@ -382,11 +436,22 @@
     hsum_ref[pl.ds(1, groups, stride=2), :] = low
     level = (top + low) * 0.5
     pk_in[band] = pk_out[...]
+
+    for i in range(1, bands):
+        slot = lax.rem(band + bands - i, bands)
+        m_copy(slot, slot).wait_recv()
+    lane = lax.broadcasted_iota(jnp.int32, (slots, LANES), 1)
+    slot_id = lax.broadcasted_iota(jnp.int32, (slots, LANES), 0)
+    marks = []
+    for d in range(bands):
+        spread_row = jnp.broadcast_to(mk_in[d], (slots, LANES))
+        column = jnp.sum(jnp.where(lane == slot_id, spread_row, 0.0), axis=1, keepdims=True)
+        marks.append(jnp.broadcast_to(column, (slots, LANES)).astype(jnp.int32))
+
     for i in range(1, bands):
         slot = lax.rem(band + bands - i, bands)
         p_copy(slot, slot).wait_recv()
-    for d in range(bands):
-        diff_ref[d] = pk_in[d] - level
+    sift(bands, groups, slots, [pk_in[d] - level for d in range(bands)], marks, out_ref)
 
     for peer in others:
         x_copy(peer, me).wait_send()
@@ -406,31 +471,6 @@
     for peer in other_bands:
         m_copy(peer, band).wait_send()
         p_copy(peer, band).wait_send()
-
-
-def sift_kernel(bands, hsum_ref, diff_ref, mark_ref, out_h_ref, out_ref):
-    out_h_ref[...] = hsum_ref[...]
-    groups = diff_ref.shape[1]
-    slots = mark_ref.shape[1]
-    lane = lax.broadcasted_iota(jnp.int32, (slots, LANES), 1)
-    for d in range(bands):
-        mark = mark_ref[d].astype(jnp.int32)
-        begin = jnp.maximum(mark, 0)
-        row, shift = begin >> 7, begin & (LANES - 1)
-        parts = [p.astype(jnp.float32) for p in split_exactly(diff_ref[d])]
-        parts.append(jnp.zeros((LANES - 3 * groups, LANES), jnp.float32))
-        source = jnp.concatenate(parts, axis=0).astype(jnp.bfloat16)
-        live = lane < 3 * groups
-        wanted = lane & (groups - 1)
-        first = jnp.where(live & (wanted == row), 1.0, 0.0)
-        second = jnp.where(live & (wanted == row + 1), 1.0, 0.0)
-        choose = jnp.concatenate([first, second], axis=0).astype(jnp.bfloat16)
-        pair = dot(choose, source, ((1,), (0,)))
-        index = (lane + shift) & (LANES - 1)
-        low = jnp.take_along_axis(pair[:slots], index, axis=1, mode="promise_in_bounds")
-        high = jnp.take_along_axis(pair[slots:], index, axis=1, mode="promise_in_bounds")
-        value = jnp.where(lane + shift < LANES, low, high)
-        out_ref[d] = jnp.where(mark >= 0, value, 0.0)
 
 
 def per_device(series, cand_start, cand_count):
@@ -448,17 +488,18 @@
     vmem = pl.BlockSpec(memory_space=pltpu.VMEM)
     hbm = pl.BlockSpec(memory_space=pl.ANY)
     dma = pltpu.SemaphoreType.DMA
-    hsum, diff, mark = pl.pallas_call(
+    hsum, sifted = pl.pallas_call(
         functools.partial(search_kernel, shards, bands, tuple(offsets), total),
         name="search",
         out_shape=(
             jax.ShapeDtypeStruct((dm_rows * groups, LANES), f32),
-            jax.ShapeDtypeStruct((bands, groups, LANES), f32),
-            jax.ShapeDtypeStruct((bands, slots, LANES), f32),
+            jax.ShapeDtypeStruct((bands, slots, BW), f32),
         ),
-        in_specs=[hbm, vmem, pl.BlockSpec(memory_space=pltpu.SMEM), hbm],
-        out_specs=[vmem] * 3,
+        in_specs=[hbm] * 4,
+        out_specs=[vmem] * 2,
         scratch_shapes=[
+            pltpu.VMEM((bands, slots), jnp.int32),
+            pltpu.SMEM((bands,), jnp.int32),
             pltpu.VMEM(tab.shape, f32),
             pltpu.VMEM((shards, dm_rows * chunks // shards, LANES), f32),
             pltpu.VMEM((shards, 2, LEFT // shards, RIGHT), f32),
@@ -480,23 +521,15 @@
             pltpu.VMEM((bands, groups, LANES), f32),
             *[dma((shards,)) for _ in range(8)],
             *[dma((bands,)) for _ in range(4)],
-            dma((2,)),
+            dma((4,)),
+            pltpu.SemaphoreType.REGULAR,
+            pltpu.SemaphoreType.REGULAR,
         ],
         compiler_params=pltpu.CompilerParams(
-            collective_id=0, has_side_effects=True, vmem_limit_bytes=32 << 20
+            collective_id=0, has_side_effects=True, vmem_limit_bytes=60 << 20
         ),
     )(x, cand_start.reshape(bands, slots), cand_count.reshape(bands), jnp.asarray(tab))
-    harmonic, sifted = pl.pallas_call(
-        functools.partial(sift_kernel, bands),
-        name="sift",
-        out_shape=(
-            jax.ShapeDtypeStruct(hsum.shape, f32),
-            jax.ShapeDtypeStruct((bands, slots, BW), f32),
-        ),
-        in_specs=[vmem] * 3,
-        out_specs=[vmem] * 2,
-    )(hsum, diff, mark)
-    harmonic = harmonic.reshape(groups, dm_rows, LANES).transpose(1, 0, 2)
+    harmonic = hsum.reshape(groups, dm_rows, LANES).transpose(1, 0, 2)
     return harmonic.reshape(dm_rows, fundamentals), sifted[None, None]
 
 

time: 58.2 us -> 50.9 us (0.87)
  Pallas kernels: 52.3 us -> 47.3 us
  local copies, waits for them, and re-layouts: 4.58 us -> 2.8 us
    pallas_call x1, Pallas kernels: 50.5 us -> 47.3 us  [per_device(): pl.pallas_call(functools.partial(search_kernel, shards, bands, tuple(offs...]
    pallas_call x1 -> x0, Pallas kernels: 1.79 us -> none  [per_device(): pl.pallas_call(functools.partial(sift_kernel, bands), name='sift', out_sh...]
    unnamed x14 -> x2, local copies, waits for them, and re-layouts: 4.58 us -> 2.8 us
where the time goes in v1:
time: 50.9 us; the launch traced here: 50.7 us
  Pallas kernels  47.3 us (93%)
  local copies, waits for them, and re-layouts  2.8 us (6%)
  between operations  0.64 us (1%)
    pallas_call x1, Pallas kernels, per_device(): pl.pallas_call(functools.partial(search_kernel, shards, bands, tuple(offs...  47.3 us
    unnamed x2, local copies, waits for them, and re-layouts  2.8 us

profile of v1, /device:TPU:513, one launch (start us, length us, event | category | flops | bytes accessed | tf_op | source)
XLA Modules:
  0.0 50.7 jit_solution(74620344367895575)
XLA Ops:
  0.6 47.3 %search.1 = (f32[32,128]{1,0:T(8,128)}, f32[8,16,128]{2,1,0:T(8,128)}) custom-call(f32[512,128]{1,0:T(8,128)} %bitcast.13, s32[8,16]{1,0:T(8,128)} %bitcast.16, s32[8]{0:T(128)} %bitcast.17, f32[1376,128]{1,0:T(8,128)} %constant.2.clone.tab_hbm), custom_call_target="tpu_custom_call" | custom-call | tf_op jit(solution)/shard_map/search/pallas_call | solution.py:491
  47.9 1.3 %copy.10 = f32[2,2048]{1,0:T(2,128)} copy(f32[2,2048]{1,0:T(2,128)} %bitcast.15) | data formatting | bytes 32768
  49.2 1.5 %copy.11 = f32[1,1,8,16,128]{4,3,2,1,0:T(8,128)} copy(f32[1,1,8,16,128]{4,3,2,1,0:T(8,128)} %bitcast.14) | data formatting | bytes 131072

commit v2 on v1

--- a/solution.py
+++ b/solution.py
@@ -145,29 +145,32 @@
     bins = total // 2
     x_rows = x_in.shape[1]
 
-    first_shard, first_band = me == 0, band == 0
     barrier = pltpu.get_barrier_semaphore()
     others = [lax.rem(me + i, shards) for i in far_first(shards)]
     other_bands = [lax.rem(band + i, bands) for i in far_first(bands)]
 
-    def greet(semaphore, axis, peers):
-        for peer in peers:
+    def rank(index, count):
+        return jnp.where(index == 0, count, index)
+
+    my_rank, band_rank = rank(me, shards), rank(band, bands)
+
+    def greet(semaphore, axis, peer, wanted):
+        @pl.when(wanted)
+        def _():
             pl.semaphore_signal(semaphore, inc=1, device_id={axis: peer}, device_id_type=MESH)
 
-    @pl.when(jnp.logical_not(first_shard))
+    for peer in others:
+        greet(barrier, "tm", peer, rank(peer, shards) > my_rank)
+    for peer in other_bands:
+        greet(barrier, "dm", peer, rank(peer, bands) > band_rank)
+    lowers = my_rank + band_rank - 2
+
+    @pl.when(lowers > 0)
     def _():
-        greet(barrier, "tm", others)
-
-    @pl.when(jnp.logical_not(first_band))
-    def _():
-        greet(barrier, "dm", other_bands)
-
-    late = first_shard.astype(jnp.int32) + first_band.astype(jnp.int32)
-    pl.semaphore_wait(barrier, shards + bands - 4 + late)
-
-    @pl.when(first_shard)
-    def _():
-        greet(here_shard, "tm", others)
+        pl.semaphore_wait(barrier, lowers)
+
+    for peer in others:
+        greet(here_shard.at[me], "tm", peer, rank(peer, shards) < my_rank)
 
     def remote(src, dst, send, recv, axis, peer):
         return pltpu.make_async_remote_copy(
@@ -200,7 +203,7 @@
 
     for peer in others:
 
-        @pl.when(peer != 0)
+        @pl.when(rank(peer, shards) < my_rank)
         def _(peer=peer):
             x_copy(peer, me).start()
 
@@ -214,14 +217,15 @@
     get_tab = pltpu.make_async_copy(tab_hbm, tab, local_sem.at[3])
     get_tab.start()
 
-    @pl.when(first_band)
-    def _():
-        greet(here_band, "dm", other_bands)
-
-    @pl.when(jnp.logical_not(first_shard))
-    def _():
-        pl.semaphore_wait(here_shard, 1)
-        x_copy(0, me).start()
+    for peer in other_bands:
+        greet(here_band.at[band], "dm", peer, rank(peer, bands) < band_rank)
+    for i in range(1, shards):
+        peer = lax.rem(me + i, shards)
+
+        @pl.when(rank(peer, shards) > my_rank)
+        def _(peer=peer):
+            pl.semaphore_wait(here_shard.at[peer], 1)
+            x_copy(peer, me).start()
 
     slots = start_ref.shape[1]
     get_starts.wait()
@@ -233,12 +237,6 @@
     lane_row = lax.broadcasted_iota(jnp.int32, (1, LANES), 1)
     for d in range(bands):
         mk_out[d] = jnp.where(lane_row < count_ref[d], starts[d : d + 1], -1.0)
-    for peer in other_bands:
-
-        @pl.when(peer != 0)
-        def _(peer=peer):
-            m_copy(peer, band).start()
-
     mk_in[band] = mk_out[band]
 
     get_tab.wait()
@@ -306,11 +304,6 @@
         y_copy(peer, me).start()
     y_in[:, pl.ds(pl.multiple_of(me * 8, 8), 8), :] = y_out[me]
 
-    @pl.when(jnp.logical_not(first_band))
-    def _():
-        pl.semaphore_wait(here_band, 1)
-        m_copy(0, band).start()
-
     for i in range(1, shards):
         slot = lax.rem(me + shards - i, shards)
         y_copy(slot, slot).wait_recv()
@@ -391,6 +384,14 @@
     for peer in others:
         s_copy(peer, me).start()
     st_in[me] = st_out[...]
+
+    for peer in other_bands:
+
+        @pl.when(rank(peer, bands) > band_rank)
+        def _(peer=peer):
+            pl.semaphore_wait(here_band.at[peer], 1)
+
+        m_copy(peer, band).start()
 
     for v in range(shards):
 
@@ -448,28 +449,30 @@
         column = jnp.sum(jnp.where(lane == slot_id, spread_row, 0.0), axis=1, keepdims=True)
         marks.append(jnp.broadcast_to(column, (slots, LANES)).astype(jnp.int32))
 
+    for peer in others:
+        x_copy(peer, me).wait_send()
+        y_copy(peer, me).wait_send()
+        s_copy(peer, me).wait_send()
+
+    @pl.when(odd)
+    def _():
+        for peer in others:
+            h_copy(peer, me, HALF).wait_send()
+
+    @pl.when(jnp.logical_not(odd))
+    def _():
+        for peer in others:
+            h_copy(peer, me, 2 * HALF).wait_send()
+
+    for peer in other_bands:
+        m_copy(peer, band).wait_send()
+
     for i in range(1, bands):
         slot = lax.rem(band + bands - i, bands)
         p_copy(slot, slot).wait_recv()
     sift(bands, groups, slots, [pk_in[d] - level for d in range(bands)], marks, out_ref)
 
-    for peer in others:
-        x_copy(peer, me).wait_send()
-        y_copy(peer, me).wait_send()
-        s_copy(peer, me).wait_send()
-
-    @pl.when(odd)
-    def _():
-        for peer in others:
-            h_copy(peer, me, HALF).wait_send()
-
-    @pl.when(jnp.logical_not(odd))
-    def _():
-        for peer in others:
-            h_copy(peer, me, 2 * HALF).wait_send()
-
     for peer in other_bands:
-        m_copy(peer, band).wait_send()
         p_copy(peer, band).wait_send()
 
 
@@ -486,7 +489,7 @@
     groups = fundamentals // LANES
     f32, bf16 = jnp.float32, jnp.bfloat16
     vmem = pl.BlockSpec(memory_space=pltpu.VMEM)
-    hbm = pl.BlockSpec(memory_space=pl.ANY)
+    hbm = pl.BlockSpec(memory_space=pltpu.HBM)
     dma = pltpu.SemaphoreType.DMA
     hsum, sifted = pl.pallas_call(
         functools.partial(search_kernel, shards, bands, tuple(offsets), total),
@@ -522,13 +525,13 @@
             *[dma((shards,)) for _ in range(8)],
             *[dma((bands,)) for _ in range(4)],
             dma((4,)),
-            pltpu.SemaphoreType.REGULAR,
-            pltpu.SemaphoreType.REGULAR,
+            pltpu.SemaphoreType.REGULAR((shards,)),
+            pltpu.SemaphoreType.REGULAR((bands,)),
         ],
         compiler_params=pltpu.CompilerParams(
-            collective_id=0, has_side_effects=True, vmem_limit_bytes=60 << 20
+            collective_id=0, has_side_effects=True, vmem_limit_bytes=24 << 20
         ),
-    )(x, cand_start.reshape(bands, slots), cand_count.reshape(bands), jnp.asarray(tab))
+    )(*[pltpu.with_memory_space_constraint(a, pltpu.HBM) for a in (x, cand_start.reshape(bands, slots), cand_count.reshape(bands), jnp.asarray(tab))])
     harmonic = hsum.reshape(groups, dm_rows, LANES).transpose(1, 0, 2)
     return harmonic.reshape(dm_rows, fundamentals), sifted[None, None]
 

time: 50.9 us -> 49 us (0.963)
  local copies, waits for them, and re-layouts: 2.8 us -> 1.24 us
    unnamed x2, local copies, waits for them, and re-layouts: 2.8 us -> 1.24 us
where the time goes in v2:
time: 49 us; the launch traced here: 48.9 us
  Pallas kernels  47 us (96%)
  local copies, waits for them, and re-layouts  1.24 us (3%)
  between operations  0.64 us (1%)
    pallas_call x1, Pallas kernels, per_device(): pl.pallas_call(functools.partial(search_kernel, shards, bands, tuple(offs...  47 us
    unnamed x2, local copies, waits for them, and re-layouts  1.24 us

profile of v2, /device:TPU:513, one launch (start us, length us, event | category | flops | bytes accessed | tf_op | source)
XLA Modules:
  0.0 48.9 jit_solution(5635878534601282925)
XLA Ops:
  0.6 47.0 %search.1 = (f32[32,128]{1,0:T(8,128)S(1)}, f32[8,16,128]{2,1,0:T(8,128)S(1)}) custom-call(f32[512,128]{1,0:T(8,128)} %bitcast.15, s32[8,16]{1,0:T(8,128)} %bitcast.16, s32[8]{0:T(128)} %bitcast.17, f32[1376,128]{1,0:T(8,128)} %constant.2.clone.tab_hbm), custom_call_target="tpu_custom_call" | custom-call | tf_op jit(solution)/shard_map/search/pallas_call | solution.py:494
  47.6 0.6 %copy.10 = f32[2,2048]{1,0:T(2,128)} copy(f32[2,2048]{1,0:T(2,128)S(1)} %bitcast.14) | data formatting | bytes 32768
  48.2 0.6 %copy.11 = f32[1,1,8,16,128]{4,3,2,1,0:T(8,128)} copy(f32[1,1,8,16,128]{4,3,2,1,0:T(8,128)S(1)} %bitcast.13) | data formatting | bytes 131072

commit v3 on v2

--- a/solution.py
+++ b/solution.py
@@ -137,7 +137,8 @@
     start_ref, count_ref, tab, x_in, y_out, y_in, w_hi, w_lo, g_hi, g_lo, t_cos, t_sin, pw,
     h_out, h_in, st_out, st_in, mk_out, mk_in, pk_out, pk_in,
     send_x, recv_x, send_y, recv_y, send_h, recv_h, send_s, recv_s,
-    send_m, recv_m, send_p, recv_p, local_sem, here_shard, here_band,
+    send_m, recv_m, send_p, recv_p, local_sem,
+    z_in, z_out, f_out, f_in, send_z, recv_z, send_w, send_f, recv_f, here_shard, here_band,
 ):
     me = lax.axis_index("tm")
     band = lax.axis_index("dm")
@@ -146,13 +147,17 @@
     x_rows = x_in.shape[1]
 
     barrier = pltpu.get_barrier_semaphore()
+    stand = shards // 2
     others = [lax.rem(me + i, shards) for i in far_first(shards)]
     other_bands = [lax.rem(band + i, bands) for i in far_first(bands)]
 
     def rank(index, count):
         return jnp.where(index == 0, count, index)
 
-    my_rank, band_rank = rank(me, shards), rank(band, bands)
+    def band_order(index):
+        return jnp.where((index == 0) & (me == 0), bands, index)
+
+    my_rank, band_rank = rank(me, shards), band_order(band)
 
     def greet(semaphore, axis, peer, wanted):
         @pl.when(wanted)
@@ -162,8 +167,8 @@
     for peer in others:
         greet(barrier, "tm", peer, rank(peer, shards) > my_rank)
     for peer in other_bands:
-        greet(barrier, "dm", peer, rank(peer, bands) > band_rank)
-    lowers = my_rank + band_rank - 2
+        greet(barrier, "dm", peer, band_order(peer) > band_rank)
+    lowers = my_rank - 1 + band_rank - jnp.where(me == 0, 1, 0)
 
     @pl.when(lowers > 0)
     def _():
@@ -185,6 +190,17 @@
     def y_copy(peer, slot):
         rows = pl.ds(pl.multiple_of(slot * 8, 8), 8)
         return remote(y_out.at[peer], y_in.at[:, rows], send_y.at[peer], recv_y.at[slot], "tm", peer)
+
+    def z_copy(slot):
+        rows = pl.ds(0, x_rows)
+        return remote(x_ref.at[rows], z_in.at[slot], send_z.at[0], recv_z.at[slot], "tm", stand)
+
+    def w_copy(peer):
+        rows = pl.ds(0, 8)
+        return remote(z_out.at[peer], y_in.at[:, rows], send_w.at[peer], recv_y.at[0], "tm", peer)
+
+    def f_copy(peer):
+        return remote(f_out.at[lax.rem(peer, 2)], f_in, send_f.at[peer], recv_f.at[0], "tm", peer)
 
     def h_copy(peer, slot, rows):
         part = pl.ds(0, rows)
@@ -218,14 +234,29 @@
     get_tab.start()
 
     for peer in other_bands:
-        greet(here_band.at[band], "dm", peer, rank(peer, bands) < band_rank)
+        greet(here_band.at[band], "dm", peer, band_order(peer) < band_rank)
     for i in range(1, shards):
         peer = lax.rem(me + i, shards)
 
-        @pl.when(rank(peer, shards) > my_rank)
+        @pl.when((rank(peer, shards) > my_rank) & (peer != 0))
         def _(peer=peer):
             pl.semaphore_wait(here_shard.at[peer], 1)
             x_copy(peer, me).start()
+
+    @pl.when((me != 0) & (me != stand))
+    def _():
+        z_copy(me).start()
+
+    @pl.when(me == 0)
+    def _():
+        own_x.wait()
+        for row in range(2):
+            for side in range(RIGHT // LANES):
+                pick = pl.ds(2 * side + row, 8, stride=4)
+                f_out[row, :, side * LANES : (side + 1) * LANES] = x_in[0, pick, :]
+        for peer in others:
+            f_copy(peer).start()
+        f_in[...] = f_out[0]
 
     slots = start_ref.shape[1]
     get_starts.wait()
@@ -287,26 +318,66 @@
         g_hi[LEFT * i : LEFT * (i + 1), :] = high
         g_lo[LEFT * i : LEFT * (i + 1), :] = low
 
-    own_x.wait()
-    for i in range(1, shards):
-        slot = lax.rem(me + shards - i, shards)
-        x_copy(slot, slot).wait_recv()
-    for row in range(2):
-        for side in range(RIGHT // LANES):
-            pick = pl.ds(2 * side + row, 8, stride=4)
-            terms = radix_transform([x_in[t, pick, :] for t in range(shards)])
-            lanes = slice(side * LANES, (side + 1) * LANES)
-            for j in range(JOBS):
-                re, im = (terms[0][0], terms[JOBS][0]) if j == 0 else terms[j]
-                y_out[2 * j + row, 0, :, lanes] = re
-                y_out[2 * j + row, 1, :, lanes] = im
-    for peer in others:
-        y_copy(peer, me).start()
-    y_in[:, pl.ds(pl.multiple_of(me * 8, 8), 8), :] = y_out[me]
-
-    for i in range(1, shards):
-        slot = lax.rem(me + shards - i, shards)
-        y_copy(slot, slot).wait_recv()
+    def across(source, first, target):
+        for row in range(2):
+            for side in range(RIGHT // LANES):
+                pick = pl.ds(2 * side + row, 8, stride=4)
+                arrays = [source[t, pick, :] for t in range(first, shards)]
+                if first:
+                    arrays = [jnp.zeros_like(arrays[0])] * first + arrays
+                terms = radix_transform(arrays)
+                lanes = slice(side * LANES, (side + 1) * LANES)
+                for j in range(JOBS):
+                    re, im = (terms[0][0], terms[JOBS][0]) if j == 0 else terms[j]
+                    target[2 * j + row, 0, :, lanes] = re
+                    target[2 * j + row, 1, :, lanes] = im
+
+    @pl.when(me == stand)
+    def _():
+        own_z = pltpu.make_async_copy(x_ref.at[pl.ds(0, x_rows)], z_in.at[stand], local_sem.at[4])
+        own_z.start()
+        own_z.wait()
+        for t in range(1, shards):
+            if t != stand:
+                z_copy(t).wait_recv()
+        across(z_in, 1, z_out)
+        for peer in range(1, shards):
+            if peer != stand:
+                w_copy(peer).start()
+        y_in[:, :8, :] = z_out[stand]
+
+    @pl.when(me != 0)
+    def _():
+        own_x.wait()
+        for i in range(1, shards):
+            slot = lax.rem(me + shards - i, shards)
+            x_copy(slot, slot).wait_recv()
+        across(x_in, 0, y_out)
+        pl.semaphore_wait(here_shard.at[0], 1)
+        for peer in others:
+            y_copy(peer, me).start()
+        y_in[:, pl.ds(pl.multiple_of(me * 8, 8), 8), :] = y_out[me]
+
+    @pl.when(me == stand)
+    def _():
+        w_copy(0).start()
+
+    @pl.when(me != 0)
+    def _():
+        f_copy(0).wait_recv()
+
+    @pl.when(me != stand)
+    def _():
+        w_copy(0).wait_recv()
+
+    for u in range(1, shards):
+
+        @pl.when(me != u)
+        def _(u=u):
+            y_copy(u, u).wait_recv()
+
+    y_in[0, :8, :] = y_in[0, :8, :] + f_in[...]
+    y_in[1, :8, :] = y_in[1, :8, :] + alone * f_in[...]
 
     y = jnp.concatenate([y_in[0], y_in[1]], axis=0)
     u = dot_split((w_hi[...], w_lo[...]), split(y), ((1,), (0,)))
@@ -387,7 +458,7 @@
 
     for peer in other_bands:
 
-        @pl.when(rank(peer, bands) > band_rank)
+        @pl.when(band_order(peer) > band_rank)
         def _(peer=peer):
             pl.semaphore_wait(here_band.at[peer], 1)
 
@@ -450,9 +521,32 @@
         marks.append(jnp.broadcast_to(column, (slots, LANES)).astype(jnp.int32))
 
     for peer in others:
-        x_copy(peer, me).wait_send()
-        y_copy(peer, me).wait_send()
+
+        @pl.when(peer != 0)
+        def _(peer=peer):
+            x_copy(peer, me).wait_send()
+
         s_copy(peer, me).wait_send()
+
+    @pl.when(me != 0)
+    def _():
+        for peer in others:
+            y_copy(peer, me).wait_send()
+
+    @pl.when((me != 0) & (me != stand))
+    def _():
+        z_copy(me).wait_send()
+
+    @pl.when(me == stand)
+    def _():
+        for peer in range(shards):
+            if peer != stand:
+                w_copy(peer).wait_send()
+
+    @pl.when(me == 0)
+    def _():
+        for peer in others:
+            f_copy(peer).wait_send()
 
     @pl.when(odd)
     def _():
@@ -524,7 +618,16 @@
             pltpu.VMEM((bands, groups, LANES), f32),
             *[dma((shards,)) for _ in range(8)],
             *[dma((bands,)) for _ in range(4)],
-            dma((4,)),
+            dma((5,)),
+            pltpu.VMEM((shards, dm_rows * chunks // shards, LANES), f32),
+            pltpu.VMEM((shards, 2, LEFT // shards, RIGHT), f32),
+            pltpu.VMEM((2, LEFT // shards, RIGHT), f32),
+            pltpu.VMEM((LEFT // shards, RIGHT), f32),
+            dma((1,)),
+            dma((shards,)),
+            dma((shards,)),
+            dma((shards,)),
+            dma((1,)),
             pltpu.SemaphoreType.REGULAR((shards,)),
             pltpu.SemaphoreType.REGULAR((bands,)),
         ],

time: 49 us -> 49.4 us (level)
  no operation moved by 1% of the time
where the time goes in v3:
time: 49.4 us; the launch traced here: 49.2 us
  Pallas kernels  47.4 us (96%)
  local copies, waits for them, and re-layouts  1.24 us (3%)
  between operations  0.64 us (1%)
    pallas_call x1, Pallas kernels, per_device(): pl.pallas_call(functools.partial(search_kernel, shards, bands, tuple(offs...  47.4 us
    unnamed x2, local copies, waits for them, and re-layouts  1.24 us

profile of v3, /device:TPU:513, one launch (start us, length us, event | category | flops | bytes accessed | tf_op | source)
XLA Modules:
  0.0 49.2 jit_solution(13382023211239198064)
XLA Ops:
  0.6 47.4 %search.1 = (f32[32,128]{1,0:T(8,128)S(1)}, f32[8,16,128]{2,1,0:T(8,128)S(1)}) custom-call(f32[512,128]{1,0:T(8,128)} %bitcast.15, s32[8,16]{1,0:T(8,128)} %bitcast.16, s32[8]{0:T(128)} %bitcast.17, f32[1376,128]{1,0:T(8,128)} %constant.2.clone.tab_hbm), custom_call_target="tpu_custom_call" | custom-call | tf_op jit(solution)/shard_map/search/pallas_call | solution.py:588
  48.0 0.6 %copy.10 = f32[2,2048]{1,0:T(2,128)} copy(f32[2,2048]{1,0:T(2,128)S(1)} %bitcast.14) | data formatting | bytes 32768
  48.6 0.6 %copy.11 = f32[1,1,8,16,128]{4,3,2,1,0:T(8,128)} copy(f32[1,1,8,16,128]{4,3,2,1,0:T(8,128)S(1)} %bitcast.13) | data formatting | bytes 131072

commit v4 on v3

--- a/solution.py
+++ b/solution.py
@@ -151,8 +151,11 @@
     others = [lax.rem(me + i, shards) for i in far_first(shards)]
     other_bands = [lax.rem(band + i, bands) for i in far_first(bands)]
 
+    first_row = band == 0
+    handles = (me != 0) | jnp.logical_not(first_row)
+
     def rank(index, count):
-        return jnp.where(index == 0, count, index)
+        return jnp.where((index == 0) & first_row, count, index)
 
     def band_order(index):
         return jnp.where((index == 0) & (me == 0), bands, index)
@@ -168,7 +171,7 @@
         greet(barrier, "tm", peer, rank(peer, shards) > my_rank)
     for peer in other_bands:
         greet(barrier, "dm", peer, band_order(peer) > band_rank)
-    lowers = my_rank - 1 + band_rank - jnp.where(me == 0, 1, 0)
+    lowers = my_rank + band_rank - jnp.where(first_row, 1, 0) - jnp.where(me == 0, 1, 0)
 
     @pl.when(lowers > 0)
     def _():
@@ -243,11 +246,11 @@
             pl.semaphore_wait(here_shard.at[peer], 1)
             x_copy(peer, me).start()
 
-    @pl.when((me != 0) & (me != stand))
+    @pl.when(first_row & (me != 0) & (me != stand))
     def _():
         z_copy(me).start()
 
-    @pl.when(me == 0)
+    @pl.when(first_row & (me == 0))
     def _():
         own_x.wait()
         for row in range(2):
@@ -332,7 +335,7 @@
                     target[2 * j + row, 0, :, lanes] = re
                     target[2 * j + row, 1, :, lanes] = im
 
-    @pl.when(me == stand)
+    @pl.when(first_row & (me == stand))
     def _():
         own_z = pltpu.make_async_copy(x_ref.at[pl.ds(0, x_rows)], z_in.at[stand], local_sem.at[4])
         own_z.start()
@@ -346,27 +349,31 @@
                 w_copy(peer).start()
         y_in[:, :8, :] = z_out[stand]
 
-    @pl.when(me != 0)
+    @pl.when(handles)
     def _():
         own_x.wait()
         for i in range(1, shards):
             slot = lax.rem(me + shards - i, shards)
             x_copy(slot, slot).wait_recv()
         across(x_in, 0, y_out)
-        pl.semaphore_wait(here_shard.at[0], 1)
+
+        @pl.when(first_row)
+        def _():
+            pl.semaphore_wait(here_shard.at[0], 1)
+
+        @pl.when(first_row & (me == stand))
+        def _():
+            w_copy(0).start()
+
         for peer in others:
             y_copy(peer, me).start()
         y_in[:, pl.ds(pl.multiple_of(me * 8, 8), 8), :] = y_out[me]
 
-    @pl.when(me == stand)
-    def _():
-        w_copy(0).start()
-
-    @pl.when(me != 0)
+    @pl.when(first_row & (me != 0))
     def _():
         f_copy(0).wait_recv()
 
-    @pl.when(me != stand)
+    @pl.when(me != jnp.where(first_row, stand, 0))
     def _():
         w_copy(0).wait_recv()
 
@@ -376,8 +383,10 @@
         def _(u=u):
             y_copy(u, u).wait_recv()
 
-    y_in[0, :8, :] = y_in[0, :8, :] + f_in[...]
-    y_in[1, :8, :] = y_in[1, :8, :] + alone * f_in[...]
+    @pl.when(first_row)
+    def _():
+        y_in[0, :8, :] = y_in[0, :8, :] + f_in[...]
+        y_in[1, :8, :] = y_in[1, :8, :] + alone * f_in[...]
 
     y = jnp.concatenate([y_in[0], y_in[1]], axis=0)
     u = dot_split((w_hi[...], w_lo[...]), split(y), ((1,), (0,)))
@@ -522,28 +531,28 @@
 
     for peer in others:
 
-        @pl.when(peer != 0)
+        @pl.when((peer != 0) | jnp.logical_not(first_row))
         def _(peer=peer):
             x_copy(peer, me).wait_send()
 
         s_copy(peer, me).wait_send()
 
-    @pl.when(me != 0)
+    @pl.when(handles)
     def _():
         for peer in others:
             y_copy(peer, me).wait_send()
 
-    @pl.when((me != 0) & (me != stand))
+    @pl.when(first_row & (me != 0) & (me != stand))
     def _():
         z_copy(me).wait_send()
 
-    @pl.when(me == stand)
+    @pl.when(first_row & (me == stand))
     def _():
         for peer in range(shards):
             if peer != stand:
                 w_copy(peer).wait_send()
 
-    @pl.when(me == 0)
+    @pl.when(first_row & (me == 0))
     def _():
         for peer in others:
             f_copy(peer).wait_send()

time: 49.4 us -> 49.7 us (level)
  no operation moved by 1% of the time
where the time goes in v4:
time: 49.7 us; the launch traced here: 49.5 us
  Pallas kernels  47.6 us (96%)
  local copies, waits for them, and re-layouts  1.24 us (2%)
  between operations  0.64 us (1%)
    pallas_call x1, Pallas kernels, per_device(): pl.pallas_call(functools.partial(search_kernel, shards, bands, tuple(offs...  47.6 us
    unnamed x2, local copies, waits for them, and re-layouts  1.24 us

profile of v4, /device:TPU:513, one launch (start us, length us, event | category | flops | bytes accessed | tf_op | source)
XLA Modules:
  0.0 49.5 jit_solution(13845377620860954852)
XLA Ops:
  0.6 47.6 %search.1 = (f32[32,128]{1,0:T(8,128)S(1)}, f32[8,16,128]{2,1,0:T(8,128)S(1)}) custom-call(f32[512,128]{1,0:T(8,128)} %bitcast.15, s32[8,16]{1,0:T(8,128)} %bitcast.16, s32[8]{0:T(128)} %bitcast.17, f32[1376,128]{1,0:T(8,128)} %constant.2.clone.tab_hbm), custom_call_target="tpu_custom_call" | custom-call | tf_op jit(solution)/shard_map/search/pallas_call | solution.py:597
  48.3 0.6 %copy.10 = f32[2,2048]{1,0:T(2,128)} copy(f32[2,2048]{1,0:T(2,128)S(1)} %bitcast.14) | data formatting | bytes 32768
  48.9 0.6 %copy.11 = f32[1,1,8,16,128]{4,3,2,1,0:T(8,128)} copy(f32[1,1,8,16,128]{4,3,2,1,0:T(8,128)S(1)} %bitcast.13) | data formatting | bytes 131072

commit v5 on v4

--- a/solution.py
+++ b/solution.py
@@ -138,7 +138,7 @@
     h_out, h_in, st_out, st_in, mk_out, mk_in, pk_out, pk_in,
     send_x, recv_x, send_y, recv_y, send_h, recv_h, send_s, recv_s,
     send_m, recv_m, send_p, recv_p, local_sem,
-    z_in, z_out, f_out, f_in, send_z, recv_z, send_w, send_f, recv_f, here_shard, here_band,
+    relay_buf, relay_sem, z_in, z_out, f_out, f_in, send_z, recv_z, send_w, send_f, recv_f, here_shard, here_band,
 ):
     me = lax.axis_index("tm")
     band = lax.axis_index("dm")
@@ -193,6 +193,19 @@
     def y_copy(peer, slot):
         rows = pl.ds(pl.multiple_of(slot * 8, 8), 8)
         return remote(y_out.at[peer], y_in.at[:, rows], send_y.at[peer], recv_y.at[slot], "tm", peer)
+
+    far, quarter = shards // 2, shards // 4
+    relay = lax.rem(me + shards - quarter, shards)
+    origin = lax.rem(me + quarter, shards)
+    origin_handles = (origin != 0) | jnp.logical_not(first_row)
+
+    def r_copy():
+        opposite = lax.rem(me + far, shards)
+        return remote(y_out.at[opposite], relay_buf, send_y.at[opposite], relay_sem.at[0], "tm", relay)
+
+    def fwd_copy():
+        rows = pl.ds(pl.multiple_of(origin * 8, 8), 8)
+        return remote(relay_buf, y_in.at[:, rows], relay_sem.at[1], recv_y.at[origin], "tm", relay)
 
     def z_copy(slot):
         rows = pl.ds(0, x_rows)
@@ -365,9 +378,15 @@
         def _():
             w_copy(0).start()
 
-        for peer in others:
-            y_copy(peer, me).start()
+        r_copy().start()
+        for i in far_first(shards)[1:]:
+            y_copy(lax.rem(me + i, shards), me).start()
         y_in[:, pl.ds(pl.multiple_of(me * 8, 8), 8), :] = y_out[me]
+
+    @pl.when(origin_handles)
+    def _():
+        r_copy().wait_recv()
+        fwd_copy().start()
 
     @pl.when(first_row & (me != 0))
     def _():
@@ -539,8 +558,13 @@
 
     @pl.when(handles)
     def _():
-        for peer in others:
-            y_copy(peer, me).wait_send()
+        r_copy().wait_send()
+        for i in far_first(shards)[1:]:
+            y_copy(lax.rem(me + i, shards), me).wait_send()
+
+    @pl.when(origin_handles)
+    def _():
+        fwd_copy().wait_send()
 
     @pl.when(first_row & (me != 0) & (me != stand))
     def _():
@@ -628,6 +652,8 @@
             *[dma((shards,)) for _ in range(8)],
             *[dma((bands,)) for _ in range(4)],
             dma((5,)),
+            pltpu.VMEM((2, LEFT // shards, RIGHT), f32),
+            dma((2,)),
             pltpu.VMEM((shards, dm_rows * chunks // shards, LANES), f32),
             pltpu.VMEM((shards, 2, LEFT // shards, RIGHT), f32),
             pltpu.VMEM((2, LEFT // shards, RIGHT), f32),

time: 49.7 us -> 50.2 us (1.010)
    pallas_call x1, Pallas kernels: 47.6 us -> 48.1 us  [per_device(): pl.pallas_call(functools.partial(search_kernel, shards, bands, tuple(offs...]
where the time goes in v5:
time: 50.2 us; the launch traced here: 50 us
  Pallas kernels  48.1 us (96%)
  local copies, waits for them, and re-layouts  1.24 us (2%)
  between operations  0.64 us (1%)
    pallas_call x1, Pallas kernels, per_device(): pl.pallas_call(functools.partial(search_kernel, shards, bands, tuple(offs...  48.1 us
    unnamed x2, local copies, waits for them, and re-layouts  1.24 us

profile of v5, /device:TPU:513, one launch (start us, length us, event | category | flops | bytes accessed | tf_op | source)
XLA Modules:
  0.0 50.0 jit_solution(679500603595177993)
XLA Ops:
  0.6 48.1 %search.1 = (f32[32,128]{1,0:T(8,128)S(1)}, f32[8,16,128]{2,1,0:T(8,128)S(1)}) custom-call(f32[512,128]{1,0:T(8,128)} %bitcast.15, s32[8,16]{1,0:T(8,128)} %bitcast.16, s32[8]{0:T(128)} %bitcast.17, f32[1376,128]{1,0:T(8,128)} %constant.2.clone.tab_hbm), custom_call_target="tpu_custom_call" | custom-call | tf_op jit(solution)/shard_map/search/pallas_call | solution.py:621
  48.8 0.6 %copy.10 = f32[2,2048]{1,0:T(2,128)} copy(f32[2,2048]{1,0:T(2,128)S(1)} %bitcast.14) | data formatting | bytes 32768
  49.4 0.6 %copy.11 = f32[1,1,8,16,128]{4,3,2,1,0:T(8,128)} copy(f32[1,1,8,16,128]{4,3,2,1,0:T(8,128)S(1)} %bitcast.13) | data formatting | bytes 131072

commit v6 on v2

--- a/solution.py
+++ b/solution.py
@@ -152,7 +152,10 @@
     def rank(index, count):
         return jnp.where(index == 0, count, index)
 
-    my_rank, band_rank = rank(me, shards), rank(band, bands)
+    def band_order(index):
+        return jnp.where((index == 0) & (me == 0), bands, index)
+
+    my_rank, band_rank = rank(me, shards), band_order(band)
 
     def greet(semaphore, axis, peer, wanted):
         @pl.when(wanted)
@@ -162,8 +165,8 @@
     for peer in others:
         greet(barrier, "tm", peer, rank(peer, shards) > my_rank)
     for peer in other_bands:
-        greet(barrier, "dm", peer, rank(peer, bands) > band_rank)
-    lowers = my_rank + band_rank - 2
+        greet(barrier, "dm", peer, band_order(peer) > band_rank)
+    lowers = my_rank - 1 + band_rank - jnp.where(me == 0, 1, 0)
 
     @pl.when(lowers > 0)
     def _():
@@ -218,7 +221,7 @@
     get_tab.start()
 
     for peer in other_bands:
-        greet(here_band.at[band], "dm", peer, rank(peer, bands) < band_rank)
+        greet(here_band.at[band], "dm", peer, band_order(peer) < band_rank)
     for i in range(1, shards):
         peer = lax.rem(me + i, shards)
 
@@ -387,7 +390,7 @@
 
     for peer in other_bands:
 
-        @pl.when(rank(peer, bands) > band_rank)
+        @pl.when(band_order(peer) > band_rank)
         def _(peer=peer):
             pl.semaphore_wait(here_band.at[peer], 1)
 

time: 49 us -> 49.1 us (level)
  no operation moved by 1% of the time
where the time goes in v6:
time: 49.1 us; the launch traced here: 48.9 us
  Pallas kernels  47.1 us (96%)
  local copies, waits for them, and re-layouts  1.24 us (3%)
  between operations  0.64 us (1%)
    pallas_call x1, Pallas kernels, per_device(): pl.pallas_call(functools.partial(search_kernel, shards, bands, tuple(offs...  47.1 us
    unnamed x2, local copies, waits for them, and re-layouts  1.24 us

profile of v6, /device:TPU:513, one launch (start us, length us, event | category | flops | bytes accessed | tf_op | source)
XLA Modules:
  0.0 48.9 jit_solution(14954467612534307927)
XLA Ops:
  0.6 47.1 %search.1 = (f32[32,128]{1,0:T(8,128)S(1)}, f32[8,16,128]{2,1,0:T(8,128)S(1)}) custom-call(f32[512,128]{1,0:T(8,128)} %bitcast.15, s32[8,16]{1,0:T(8,128)} %bitcast.16, s32[8]{0:T(128)} %bitcast.17, f32[1376,128]{1,0:T(8,128)} %constant.2.clone.tab_hbm), custom_call_target="tpu_custom_call" | custom-call | tf_op jit(solution)/shard_map/search/pallas_call | solution.py:497
  47.7 0.6 %copy.10 = f32[2,2048]{1,0:T(2,128)} copy(f32[2,2048]{1,0:T(2,128)S(1)} %bitcast.14) | data formatting | bytes 32768
  48.3 0.6 %copy.11 = f32[1,1,8,16,128]{4,3,2,1,0:T(8,128)} copy(f32[1,1,8,16,128]{4,3,2,1,0:T(8,128)S(1)} %bitcast.13) | data formatting | bytes 131072

commit v7 on v6

--- a/solution.py
+++ b/solution.py
@@ -60,7 +60,8 @@
 
 def dot_split(left, right, dims):
     (lh, ll), (rh, rl) = left, right
-    return dot(lh, rh, dims) + (dot(ll, rh, dims) + dot(lh, rl, dims))
+    (la,), (ra,) = dims
+    return dot(jnp.concatenate([lh, ll, lh], axis=la), jnp.concatenate([rh, rh, rl], axis=ra), dims)
 
 
 def radix_transform(x):

time: 49.1 us -> 49.1 us (level)
  no operation moved by 1% of the time
where the time goes in v7:
time: 49.1 us; the launch traced here: 48.9 us
  Pallas kernels  47.1 us (96%)
  local copies, waits for them, and re-layouts  1.24 us (3%)
  between operations  0.64 us (1%)
    pallas_call x1, Pallas kernels, per_device(): pl.pallas_call(functools.partial(search_kernel, shards, bands, tuple(offs...  47.1 us
    unnamed x2, local copies, waits for them, and re-layouts  1.24 us

profile of v7, /device:TPU:513, one launch (start us, length us, event | category | flops | bytes accessed | tf_op | source)
XLA Modules:
  0.0 48.9 jit_solution(4790328672380765263)
XLA Ops:
  0.6 47.1 %search.1 = (f32[32,128]{1,0:T(8,128)S(1)}, f32[8,16,128]{2,1,0:T(8,128)S(1)}) custom-call(f32[512,128]{1,0:T(8,128)} %bitcast.15, s32[8,16]{1,0:T(8,128)} %bitcast.16, s32[8]{0:T(128)} %bitcast.17, f32[1376,128]{1,0:T(8,128)} %constant.2.clone.tab_hbm), custom_call_target="tpu_custom_call" | custom-call | tf_op jit(solution)/shard_map/search/pallas_call | solution.py:498
  47.7 0.6 %copy.10 = f32[2,2048]{1,0:T(2,128)} copy(f32[2,2048]{1,0:T(2,128)S(1)} %bitcast.14) | data formatting | bytes 32768
  48.3 0.6 %copy.11 = f32[1,1,8,16,128]{4,3,2,1,0:T(8,128)} copy(f32[1,1,8,16,128]{4,3,2,1,0:T(8,128)S(1)} %bitcast.13) | data formatting | bytes 131072
